TPU v7x, 256 devices: a whole 4x4x8 slice. The times are simulated.
256 devices in a mesh: gx: 16 (over x, y), gy: 8 (over z), gz: 2 (over core).
Axes of the slice: x: 4, y: 4, z: 8, core: 2. Of those that a mesh axis runs over, the one named last changes fastest.
Arguments:
- well_sources: float32 [12288, 64], P(('gx', 'gy'), 'gz'), may hold values from -6 to 6
- well_owner: int32 [12288, 1], P(('gx', 'gy')), may hold values from 0 to 127; in each aligned block of 96 rows (0 to 95, 96 to 191, ...) at most 2 rows name the same one
- well_cell: int32 [12288], P(('gx', 'gy')), may hold values from 0 to 2047
- flow_sign: int32 [3, 64, 256, 1024], P(None, 'gz', 'gx', 'gy'), may hold values from 0 to 7
- courant: float32 [3, 64, 256, 1024], P(None, 'gz', 'gx', 'gy'), may hold values from 0.01 to 0.3
- tracer: float32 [3, 64, 256, 1024], P(None, 'gz', 'gx', 'gy'), may hold values from -6 to 6
Outputs:
- lambda_start: float32 [64, 256, 1024], P('gz', 'gx', 'gy')
- smoothed: float32 [1024, 64, 256], P(('gx', 'gy', 'gz'))
Inputs may be any that keep to these rules, and one draw needn't show every extreme that they name: `well_owner`: among the wells of one index of gx+gy at most 2 name the same owner, a bound that some block of them reaches.
All inputs are finite; a program needn't handle non-finite values.
Results may differ from a plain program's by a relative error of at most 0.00015.
Values sent between devices are 32-bit elements; how exact they have to be, the bound alone decides.
No kernel may reach another device: no remote copies, remote signals or barrier semaphores. Data moves between devices by JAX's collectives and lax.ppermute only.
A program may use at most 128 MiB of HBM per device.

v0:
```python
import math
import jax
import jax.numpy as jnp
from jax import lax
from jax.sharding import PartitionSpec as P

STEPS = 3


def with_halo(block, sides, width):
    for axis, dim in sides:
        count = lax.axis_size(axis)
        forward = [(i, i + 1) for i in range(count - 1)]
        backward = [(target, source) for source, target in forward]
        low = lax.ppermute(
            lax.slice_in_dim(block, block.shape[dim] - width, None, axis=dim), axis, forward
        )
        high = lax.ppermute(lax.slice_in_dim(block, 0, width, axis=dim), axis, backward)
        block = jnp.concatenate([low, block, high], axis=dim)
    return block


def correlation(extent, length):
    places = jnp.arange(extent).astype(jnp.float32)
    spacing = jnp.abs(places[:, None] - places[None, :])
    return jnp.exp(-spacing / length) / math.sqrt(length)


def advance_weights(adjoint, rising_pad, falling_pad, staying):
    padded = with_halo(adjoint, (("gx", 1), ("gy", 2), ("gz", 0)), 1)
    updated = staying * adjoint
    updated = (
        updated
        + rising_pad[0, 1:-1, 2:, 1:-1] * padded[1:-1, 2:, 1:-1]
        + falling_pad[0, 1:-1, :-2, 1:-1] * padded[1:-1, :-2, 1:-1]
    )
    updated = (
        updated
        + rising_pad[1, 1:-1, 1:-1, 2:] * padded[1:-1, 1:-1, 2:]
        + falling_pad[1, 1:-1, 1:-1, :-2] * padded[1:-1, 1:-1, :-2]
    )
    updated = (
        updated
        + rising_pad[2, 2:, 1:-1, 1:-1] * padded[2:, 1:-1, 1:-1]
        + falling_pad[2, :-2, 1:-1, 1:-1] * padded[:-2, 1:-1, 1:-1]
    )
    return updated


def per_device(well_sources, well_owner, well_cell, flow_sign, courant, tracer):
    brick_z, brick_x, brick_y = (courant.shape[1], courant.shape[2], courant.shape[3])
    columns = brick_x * brick_y
    groups = lax.axis_size("gx") * lax.axis_size("gy")
    my_owner = lax.axis_index("gx") * lax.axis_size("gy") + lax.axis_index("gy")
    owners = well_owner[:, 0]
    all_sources, all_owner, all_cell = (
        lax.all_gather(well_sources, ("gx", "gy"), axis=0, tiled=True),
        lax.all_gather(owners, ("gx", "gy"), axis=0, tiled=True),
        lax.all_gather(well_cell, ("gx", "gy"), axis=0, tiled=True),
    )
    target = jnp.where(all_owner == my_owner, all_cell, columns)
    landed = (
        jnp.zeros((brick_z, columns), jnp.float32)
        .at[:, target]
        .add(jnp.transpose(all_sources), mode="drop")
    )
    adjoint = landed.reshape(brick_z, brick_x, brick_y)
    upward = jnp.stack([flow_sign // 1 % 2, flow_sign // 2 % 2, flow_sign // 4 % 2], axis=1).astype(
        jnp.float32
    )
    staying = 1.0 - (courant[0] + courant[1] + courant[2])
    gradient = jnp.zeros((brick_z, brick_x, brick_y), jnp.float32)
    weights = jnp.stack([courant[None] * upward, courant[None] * (1.0 - upward)])
    weight_pad = with_halo(weights, (("gx", 4), ("gy", 5), ("gz", 3)), 1)
    for step in reversed(range(STEPS)):
        adjoint = advance_weights(adjoint, weight_pad[0, step], weight_pad[1, step], staying)
        gradient = gradient + adjoint * tracer[step]
    highest = lax.Precision.HIGHEST
    y_lines = lax.all_to_all(gradient, "gy", split_axis=1, concat_axis=2, tiled=True)
    x_share = y_lines.shape[1]
    full_y = y_lines.shape[2]
    line_count = y_lines.shape[0] * x_share
    smooth_y = lax.dot_general(
        correlation(full_y, 2 * brick_y),
        y_lines.reshape(line_count, full_y),
        (((1,), (1,)), ((), ())),
        precision=highest,
        preferred_element_type=jnp.float32,
    )
    planes = lax.all_to_all(
        lax.all_to_all(smooth_y, ("gx", "gy"), split_axis=0, concat_axis=1, tiled=True),
        "gz",
        split_axis=0,
        concat_axis=1,
        tiled=True,
    )
    y_rows = planes.shape[0]
    depth_groups = lax.axis_size("gz")
    plane_view = planes.reshape(y_rows, depth_groups, groups, brick_z, x_share)
    full_x = groups * x_share
    table_x = correlation(full_x, 2 * brick_x).reshape(full_x, groups, x_share)
    smooth_x = jnp.einsum("ykdza,jda->ykzj", plane_view, table_x, precision=highest)
    full_z = depth_groups * brick_z
    smooth_x = smooth_x.reshape(y_rows, full_z, full_x)
    smoothed = jnp.einsum(
        "yzj,iz->yij", smooth_x, correlation(full_z, 2 * brick_z), precision=highest
    )
    return (adjoint, smoothed)


def solution(mesh):
    return jax.shard_map(
        per_device,
        mesh=mesh,
        in_specs=(
            P(("gx", "gy"), "gz"),
            P(("gx", "gy"), None),
            P(("gx", "gy")),
            P(None, "gz", "gx", "gy"),
            P(None, "gz", "gx", "gy"),
            P(None, "gz", "gx", "gy"),
        ),
        out_specs=(P("gz", "gx", "gy"), P(("gx", "gy", "gz"), None, None)),
        check_vma=False,
    )
```

profile of v0, /device:TPU:1, one launch (start us, length us, event | category | flops | bytes accessed | tf_op | source)
XLA Modules:
  0.0 618.9 jit_solution(1753815041108908470)
XLA Ops:
  24.7 4.7 collective-permute-done
  35.9 6.3 %fusion.95 = (f32[2,3,3,32,18,1]{5,3,4,2,1,0:T(8,128)}, f32[2,3,3,32,18,1]{5,3,4,2,1,0:T(8,128)}) fusion(f32[2,3,3,32,18,128]{5,3,4,2,1,0:T(8,128)S(1)} %pad_maximum_fusion.1), kind=kLoop, calls=%fused_computation.232 | loop fusion | bytes 165888 | tf_op jit(solution)/shard_map/slice | solution.py:16
  49.7 4.4 copy.72
  55.4 172.0 %all-reduce.5.cloned.1.call-done = (s32[12288]{0:T(1024)}, s32[12288]{0:T(1024)}) async-done(((s32[12288]{0:T(1024)}, s32[12288]{0:T(1024)}), (s32[12288]{0:T(1024)}, s32[12288]{0:T(1024)})) %all-reduce.5.cloned.1.call-update) | async-done | bytes 98320
  231.8 4.5 copy.74
  236.2 107.2 %all-gather.4.cloned.1.call-done = f32[128,96,32]{1,2,0:T(8,128)} async-done(((f32[1,96,32]{1,2,0:T(8,128)}), f32[128,96,32]{1,2,0:T(8,128)}) %all-gather.4.cloned.1.call-update) | async-done | bytes 1572880 | tf_op jit(solution)/shard_map/all_gather | solution.py:57
  343.4 5.3 copy.90
  348.7 67.0 %scatter_custom_fusion = f32[32,2048]{0,1:T(8,128)} fusion(s32[12288]{0:T(1024)S(1)} %compare_select_fusion, f32[12288,32]{1,0:T(8,128)} %bitcast.160, f32[]{:T(128)} %constant.79.clone.1), kind=kCustom, calls=%fused_computation.47 | custom fusion | flops 393216 | bytes 262656 | tf_op jit(solution)/shard_map/scatter-add | solution.py:65
  418.6 4.6 collective-permute-start.7
  423.1 6.4 %pad_maximum_fusion.7 = (f32[2,3,3,1,18,130]{5,3,4,2,1,0:T(1,128)S(1)}, f32[2,3,3,1,18,130]{5,3,4,2,1,0:T(1,128)S(1)}) fusion(f32[2,3,3,32,18,1]{5,3,4,2,1,0:T(8,128)} %copy.74, f32[2,3,3,32,18,1]{5,3,4,2,1,0:T(8,128)} %copy.73, f32[2,3,3,32,1,128]{5,3,4,2,1,0:T(8,128)} %collective-permute-done.1, f32[2,3,3,32,1,128]{5,3,4,2,1,0:T(8,128)} %copy-done.2, ...), kind=kLoop, calls=%fused_computation.55 | loop fusion | flops 421200 | bytes 5728320 | tf_op jit(solution)/shard_map/slice | solution.py:16
  430.9 8.1 %collective-permute-start.5 = (f32[2,3,3,1,18,130]{5,3,4,2,1,0:T(1,128)S(1)}, f32[2,3,3,1,18,130]{5,3,4,2,1,0:T(1,128)S(1)}, u32[]{:S(2)}, u32[]{:S(2)}) collective-permute-start(f32[2,3,3,1,18,130]{5,3,4,2,1,0:T(1,128)S(1)} %get-tuple-element.13), channel_id=1, source_target_pairs={{1,0},{3,2},{5,4},{7,6},{9,8},{11,10},{13,12},{15,14},{17,16},{19,... | collective-permute-start | bytes 505448 | tf_op jit(solution)/shard_map/ppermute | solution.py:18
  444.6 17.7 %pad_maximum_fusion = f32[2,3,3,34,18,130]{5,3,4,2,1,0:T(8,128)} fusion(f32[2,3,3,1,18,130]{5,3,4,2,1,0:T(1,128)S(1)} %collective-permute-done.5, f32[2,3,3,32,18,1]{5,3,4,2,1,0:T(8,128)S(1)} %bitcast.158, f32[2,3,3,32,1,128]{5,3,4,2,1,0:T(8,128)} %collective-permute-done.1, f32[1,3,3,32,16,128]{5,3,4,2,1,0:T(8,128)S(1)} %copy-done.1, ...), kind=kLoop, calls=%fused_computation.1 | loop fusion | flops 10024560 | bytes 11456640 | tf_op jit(solution)/shard_map/concatenate | solution.py:19
  465.6 9.0 %slice_bitcast_fusion.1 = (f32[3,34,18,130]{3,1,2,0:T(8,128)S(1)}, f32[3,34,18,130]{3,1,2,0:T(8,128)}, f32[3,34,18,130]{3,1,2,0:T(8,128)}, f32[3,34,18,130]{3,1,...) fusion(f32[2,3,3,34,18,130]{5,3,4,2,1,0:T(8,128)} %pad_maximum_fusion), kind=kLoop, calls=%fused_computation.13 | loop fusion | bytes 11456640 | tf_op jit(solution)/shard_map/squeeze | solution.py:76
  493.4 5.5 collective-permute-start.16
  512.7 4.8 collective-permute-start.21
  517.5 4.4 collective-permute-done.20
  532.7 9.9 %all-to-all-start = ((f32[32,16,128]{2,0,1:T(8,128)}), f32[32,16,128]{2,0,1:T(8,128)S(1)}, u32[]{:S(2)}, u32[]{:S(2)}) async-start(f32[32,16,128]{2,0,1:T(8,128)} %get-tuple-element.8), calls=%async_computation | async-start | bytes 524288 | tf_op jit(solution)/shard_map/all_to_all | solution.py:79
  542.6 12.2 %all-to-all-done = f32[32,16,128]{2,0,1:T(8,128)S(1)} async-done(((f32[32,16,128]{2,0,1:T(8,128)}), f32[32,16,128]{2,0,1:T(8,128)S(1)}, u32[]{:S(2)}, u32[]{:S(2)}) %all-to-all-start) | async-done | bytes 262176 | tf_op jit(solution)/shard_map/all_to_all | solution.py:79
  555.1 5.0 fusion
  561.3 14.9 %all-to-all-start.1 = ((f32[128,1,512]{2,1,0:T(1,128)}), f32[128,1,512]{2,1,0:T(1,128)S(1)}, u32[]{:S(2)}, u32[]{:S(2)}) async-start(f32[128,1,512]{2,1,0:T(1,128)} %reshape.198), calls=%async_computation.1 | async-start | bytes 524288 | tf_op jit(solution)/shard_map/all_to_all | solution.py:91
  577.1 13.1 %all-to-all-done.1 = f32[128,1,512]{2,1,0:T(1,128)S(1)} async-done(((f32[128,1,512]{2,1,0:T(1,128)}), f32[128,1,512]{2,1,0:T(1,128)S(1)}, u32[]{:S(2)}, u32[]{:S(2)}) %all-to-all-start.1) | async-done | bytes 262176 | tf_op jit(solution)/shard_map/all_to_all | solution.py:91
  592.5 5.6 all_to_all.44
  598.1 5.1 copy.86
  603.2 7.2 %copy.87 = f32[4,2,32,2,128]{4,2,1,3,0:T(8,128)S(1)} copy(f32[4,2,32,2,128]{0,3,2,4,1:T(2,128)} %bitcast.159) | data formatting | bytes 524288 | tf_op jit(solution)/shard_map/ykdza,jda->ykzj/dot_general | solution.py:102
  (121 shorter events, 98.8 us)
Async XLA Ops:
  7.2 220.2 %all-reduce.5.cloned.1.call-start = ((), (), s32[]{:S(2)}) async-start(), calls=%async_computation.4 | async-start | bytes 196608
  11.5 331.9 %all-gather.4.cloned.1.call-start = ((), (), s32[]{:S(2)}) async-start(), calls=%async_computation.3 | async-start | bytes 2113536 | tf_op jit(solution)/shard_map/all_gather | solution.py:57
  19.3 10.0 %collective-permute-start = (f32[2,3,3,32,1,128]{5,3,4,2,1,0:T(8,128)}, f32[2,3,3,32,1,128]{5,3,4,2,1,0:T(8,128)S(1)}, u32[]{:S(2)}, u32[]{:S(2)}) collective-permute-start(f32[2,3,3,32,1,128]{5,3,4,2,1,0:T(8,128)} %get-tuple-element.22), channel_id=1, source_target_pairs={{0,16},{16,32},{32,48},{48,64},{64,80},{80,96},{96,112},{112,128},... | collective-permute-start | bytes 884744 | tf_op jit(solution)/shard_map/ppermute | solution.py:15
  23.3 9.9 %collective-permute-start.1 = (f32[2,3,3,32,1,128]{5,3,4,2,1,0:T(8,128)}, f32[2,3,3,32,1,128]{5,3,4,2,1,0:T(8,128)}, u32[]{:S(2)}, u32[]{:S(2)}) collective-permute-start(f32[2,3,3,32,1,128]{5,3,4,2,1,0:T(8,128)} %get-tuple-element.23), channel_id=1, source_target_pairs={{16,0},{32,16},{48,32},{64,48},{80,64},{96,80},{112,96},{128,112},... | collective-permute-start | bytes 884744 | tf_op jit(solution)/shard_map/ppermute | solution.py:18
  46.1 182.1 %collective-permute-start.2 = (f32[2,3,3,32,18,1]{3,0,5,4,2,1:T(2,128)S(1)}, f32[2,3,3,32,18,1]{3,0,5,4,2,1:T(2,128)S(1)}, u32[]{:S(2)}, u32[]{:S(2)}) collective-permute-start(f32[2,3,3,32,18,1]{3,0,5,4,2,1:T(2,128)S(1)} %copy.71), channel_id=1, source_target_pairs={{0,2},{2,4},{4,6},{6,8},{8,10},{10,12},{12,14},{1,3},{3,5},{5,7},{... | collective-permute-start | bytes 124424 | tf_op jit(solution)/shard_map/ppermute | solution.py:15
  54.1 177.7 %collective-permute-start.3 = (f32[2,3,3,32,18,1]{3,0,5,4,2,1:T(2,128)}, f32[2,3,3,32,18,1]{3,0,5,4,2,1:T(2,128)}, u32[]{:S(2)}, u32[]{:S(2)}) collective-permute-start(f32[2,3,3,32,18,1]{3,0,5,4,2,1:T(2,128)} %copy.72), channel_id=1, source_target_pairs={{2,0},{4,2},{6,4},{8,6},{10,8},{12,10},{14,12},{3,1},{5,3},{7,5},{... | collective-permute-start | bytes 124424 | tf_op jit(solution)/shard_map/ppermute | solution.py:18
  417.2 21.8 %collective-permute-start.6 = (f32[32,1,128]{2,0,1:T(8,128)S(1)}, f32[32,1,128]{2,0,1:T(8,128)S(1)}, u32[]{:S(2)}, u32[]{:S(2)}) collective-permute-start(f32[32,1,128]{2,0,1:T(8,128)S(1)} %get-tuple-element.49), channel_id=1, source_target_pairs={{16,0},{32,16},{48,32},{64,48},{80,64},{96,80},{112,96},{128,112},... | collective-permute-start | bytes 49160 | tf_op jit(solution)/shard_map/ppermute | solution.py:18
  418.6 20.4 %collective-permute-start.7 = (f32[32,1,128]{2,0,1:T(8,128)S(1)}, f32[32,1,128]{2,0,1:T(8,128)S(1)}, u32[]{:S(2)}, u32[]{:S(2)}) collective-permute-start(f32[32,1,128]{2,0,1:T(8,128)S(1)} %get-tuple-element.48), channel_id=1, source_target_pairs={{0,16},{16,32},{32,48},{48,64},{64,80},{80,96},{96,112},{112,128},... | collective-permute-start | bytes 49160 | tf_op jit(solution)/shard_map/ppermute | solution.py:15
  429.6 14.9 %collective-permute-start.4 = (f32[2,3,3,1,18,130]{5,3,4,2,1,0:T(1,128)S(1)}, f32[2,3,3,1,18,130]{5,3,4,2,1,0:T(1,128)S(1)}, u32[]{:S(2)}, u32[]{:S(2)}) collective-permute-start(f32[2,3,3,1,18,130]{5,3,4,2,1,0:T(1,128)S(1)} %get-tuple-element.12), channel_id=1, source_target_pairs={{0,1},{2,3},{4,5},{6,7},{8,9},{10,11},{12,13},{14,15},{16,17},{18,... | collective-permute-start | bytes 505448 | tf_op jit(solution)/shard_map/ppermute | solution.py:15
  430.9 13.6 %collective-permute-start.5 = (f32[2,3,3,1,18,130]{5,3,4,2,1,0:T(1,128)S(1)}, f32[2,3,3,1,18,130]{5,3,4,2,1,0:T(1,128)S(1)}, u32[]{:S(2)}, u32[]{:S(2)}) collective-permute-start(f32[2,3,3,1,18,130]{5,3,4,2,1,0:T(1,128)S(1)} %get-tuple-element.13), channel_id=1, source_target_pairs={{1,0},{3,2},{5,4},{7,6},{9,8},{11,10},{13,12},{15,14},{17,16},{19,... | collective-permute-start | bytes 505448 | tf_op jit(solution)/shard_map/ppermute | solution.py:18
  439.2 23.1 %collective-permute-start.8 = (f32[32,18,1]{2,0,1:T(8,128)S(1)}, f32[32,18,1]{2,0,1:T(8,128)S(1)}, u32[]{:S(2)}, u32[]{:S(2)}) collective-permute-start(f32[32,18,1]{2,0,1:T(8,128)S(1)} %get-tuple-element.43), channel_id=1, source_target_pairs={{2,0},{4,2},{6,4},{8,6},{10,8},{12,10},{14,12},{3,1},{5,3},{7,5},{... | collective-permute-start | bytes 6920 | tf_op jit(solution)/shard_map/ppermute | solution.py:18
  440.5 21.8 %collective-permute-start.9 = (f32[32,18,1]{2,0,1:T(8,128)S(1)}, f32[32,18,1]{2,0,1:T(8,128)S(1)}, u32[]{:S(2)}, u32[]{:S(2)}) collective-permute-start(f32[32,18,1]{2,0,1:T(8,128)S(1)} %get-tuple-element.42), channel_id=1, source_target_pairs={{0,2},{2,4},{4,6},{6,8},{8,10},{10,12},{12,14},{1,3},{3,5},{5,7},{... | collective-permute-start | bytes 6920 | tf_op jit(solution)/shard_map/ppermute | solution.py:15
  462.5 12.2 %collective-permute-start.10 = (f32[1,18,130]{2,0,1:T(1,128)S(1)}, f32[1,18,130]{2,0,1:T(1,128)S(1)}, u32[]{:S(2)}, u32[]{:S(2)}) collective-permute-start(f32[1,18,130]{2,0,1:T(1,128)S(1)} %get-tuple-element.30), channel_id=1, source_target_pairs={{1,0},{3,2},{5,4},{7,6},{9,8},{11,10},{13,12},{15,14},{17,16},{19,... | collective-permute-start | bytes 28088 | tf_op jit(solution)/shard_map/ppermute | solution.py:18
  464.3 10.3 %collective-permute-start.11 = (f32[1,18,130]{2,0,1:T(1,128)S(1)}, f32[1,18,130]{2,0,1:T(1,128)S(1)}, u32[]{:S(2)}, u32[]{:S(2)}) collective-permute-start(f32[1,18,130]{2,0,1:T(1,128)S(1)} %get-tuple-element.31), channel_id=1, source_target_pairs={{0,1},{2,3},{4,5},{6,7},{8,9},{10,11},{12,13},{14,15},{16,17},{18,... | collective-permute-start | bytes 28088 | tf_op jit(solution)/shard_map/ppermute | solution.py:15
  477.8 5.4 collective-permute-start.12
  484.2 8.2 %collective-permute-start.14 = (f32[32,18,1]{2,0,1:T(8,128)S(1)}, f32[32,18,1]{2,0,1:T(8,128)S(1)}, u32[]{:S(2)}, u32[]{:S(2)}) collective-permute-start(f32[32,18,1]{2,0,1:T(8,128)S(1)} %get-tuple-element.41), channel_id=1, source_target_pairs={{2,0},{4,2},{6,4},{8,6},{10,8},{12,10},{14,12},{3,1},{5,3},{7,5},{... | collective-permute-start | bytes 6920 | tf_op jit(solution)/shard_map/ppermute | solution.py:18
  485.5 7.6 %collective-permute-start.15 = (f32[32,18,1]{2,0,1:T(8,128)S(1)}, f32[32,18,1]{2,0,1:T(8,128)S(1)}, u32[]{:S(2)}, u32[]{:S(2)}) collective-permute-start(f32[32,18,1]{2,0,1:T(8,128)S(1)} %get-tuple-element.40), channel_id=1, source_target_pairs={{0,2},{2,4},{4,6},{6,8},{8,10},{10,12},{12,14},{1,3},{3,5},{5,7},{... | collective-permute-start | bytes 6920 | tf_op jit(solution)/shard_map/ppermute | solution.py:15
  493.4 6.8 %collective-permute-start.16 = (f32[1,18,130]{2,0,1:T(1,128)S(1)}, f32[1,18,130]{2,0,1:T(1,128)S(1)}, u32[]{:S(2)}, u32[]{:S(2)}) collective-permute-start(f32[1,18,130]{2,0,1:T(1,128)S(1)} %get-tuple-element.28), channel_id=1, source_target_pairs={{1,0},{3,2},{5,4},{7,6},{9,8},{11,10},{13,12},{15,14},{17,16},{19,... | collective-permute-start | bytes 28088 | tf_op jit(solution)/shard_map/ppermute | solution.py:18
  504.7 5.7 collective-permute-start.18
  506.0 5.2 collective-permute-start.19
  511.4 10.5 %collective-permute-start.20 = (f32[32,18,1]{2,0,1:T(8,128)S(1)}, f32[32,18,1]{2,0,1:T(8,128)S(1)}, u32[]{:S(2)}, u32[]{:S(2)}) collective-permute-start(f32[32,18,1]{2,0,1:T(8,128)S(1)} %get-tuple-element.39), channel_id=1, source_target_pairs={{2,0},{4,2},{6,4},{8,6},{10,8},{12,10},{14,12},{3,1},{5,3},{7,5},{... | collective-permute-start | bytes 6920 | tf_op jit(solution)/shard_map/ppermute | solution.py:18
  512.7 10.1 %collective-permute-start.21 = (f32[32,18,1]{2,0,1:T(8,128)S(1)}, f32[32,18,1]{2,0,1:T(8,128)S(1)}, u32[]{:S(2)}, u32[]{:S(2)}) collective-permute-start(f32[32,18,1]{2,0,1:T(8,128)S(1)} %get-tuple-element.38), channel_id=1, source_target_pairs={{0,2},{2,4},{4,6},{6,8},{8,10},{10,12},{12,14},{1,3},{3,5},{5,7},{... | collective-permute-start | bytes 6920 | tf_op jit(solution)/shard_map/ppermute | solution.py:15
  532.7 22.2 %all-to-all-start = ((f32[32,16,128]{2,0,1:T(8,128)}), f32[32,16,128]{2,0,1:T(8,128)S(1)}, u32[]{:S(2)}, u32[]{:S(2)}) async-start(f32[32,16,128]{2,0,1:T(8,128)} %get-tuple-element.8), calls=%async_computation | async-start | bytes 524288 | tf_op jit(solution)/shard_map/all_to_all | solution.py:79
  561.3 28.9 %all-to-all-start.1 = ((f32[128,1,512]{2,1,0:T(1,128)}), f32[128,1,512]{2,1,0:T(1,128)S(1)}, u32[]{:S(2)}, u32[]{:S(2)}) async-start(f32[128,1,512]{2,1,0:T(1,128)} %reshape.198), calls=%async_computation.1 | async-start | bytes 524288 | tf_op jit(solution)/shard_map/all_to_all | solution.py:91
  (17 other events, 234.9 us)
Sparse Core Ops, SparseCore 0:
  14.1 213.2 all-reduce.4
  231.1 112.2 all-gather.3
where the time goes:
time: 620 us; the launch traced here: 619 us
  waiting for transfers between devices  328 us (53%)
  other arithmetic  109 us (18%)
  starting transfers between devices  92.9 us (15%)
  local copies, waits for them, and re-layouts  61 us (10%)
  between operations  15.4 us (2%)
  matrix products  6.64 us (1%)
    unnamed x3, waiting for transfers between devices  173 us
    all_gather x1, waiting for transfers between devices, per_device(): lax.all_gather(well_sources, ('gx', 'gy'), axis=0, tiled=True)  107 us
    scatter-add x1, other arithmetic, per_device(): landed = jnp.zeros((brick_z, columns), jnp.float32).at[:, target].add(jnp...  67 us
    ppermute x12, starting transfers between devices, with_halo(): lax.ppermute(lax.slice_in_dim(block, block.shape[dim] - width, None, axis...  38.6 us
    ppermute x12, starting transfers between devices, with_halo(): lax.ppermute(lax.slice_in_dim(block, 0, width, axis=dim), axis, backward)  29.5 us
    concatenate x5, other arithmetic, with_halo(): block = jnp.concatenate([low, block, high], axis=dim)  20.4 us
    all_to_all x1, starting transfers between devices, per_device(): lax.all_to_all(smooth_y, ('gx', 'gy'), split_axis=0, concat_axis=1, tiled...  14.9 us
    unnamed x36, local copies, waits for them, and re-layouts  13.7 us
  transfers between devices with their start and end apart: 28, of which 14 were waited for; matrix products, arithmetic and copies ran while one was open for 11% of the time, Pallas kernels for 0%

commit v1 on v0

--- a/solution.py
+++ b/solution.py
@@ -54,7 +54,12 @@
     my_owner = lax.axis_index("gx") * lax.axis_size("gy") + lax.axis_index("gy")
     owners = well_owner[:, 0]
     all_sources, all_owner, all_cell = (
-        lax.all_gather(well_sources, ("gx", "gy"), axis=0, tiled=True),
+        jnp.concatenate(
+            lax.all_to_all(
+                jnp.stack([well_sources] * lax.axis_size(("gx", "gy"))), ("gx", "gy"), 0, 0
+            ),
+            axis=0,
+        ),
         lax.all_gather(owners, ("gx", "gy"), axis=0, tiled=True),
         lax.all_gather(well_cell, ("gx", "gy"), axis=0, tiled=True),
     )

time: 620 us -> 536 us (0.86)
  waiting for transfers between devices: 328 us -> 232 us
  starting transfers between devices: 92.9 us -> 107 us
    all_gather x1 -> x0, waiting for transfers between devices: 107 us -> none  [per_device(): lax.all_gather(well_sources, ('gx', 'gy'), axis=0, tiled=True)]
    all_to_all x0 -> x1, starting transfers between devices: none -> 16.9 us  [per_device(): lax.all_to_all(jnp.stack([well_sources] * lax.axis_size(('gx', 'gy'))), (...]
    unnamed x3 -> x2, waiting for transfers between devices: 173 us -> 182 us
    unnamed x36 -> x45, local copies, waits for them, and re-layouts: 13.7 us -> 5.31 us
  transfers between devices with their start and end apart: 28 -> 28, of which waited for: 14 -> 13; matrix products, arithmetic and copies ran while one was open for 11% -> 12% of each run, Pallas kernels for 0% -> 0%
where the time goes in v1:
time: 536 us; the launch traced here: 535 us
  waiting for transfers between devices  232 us (43%)
  other arithmetic  108 us (20%)
  starting transfers between devices  107 us (20%)
  local copies, waits for them, and re-layouts  60.2 us (11%)
  between operations  15.5 us (3%)
  matrix products  6.64 us (1%)
  blocking collectives  5.63 us (1%)
    unnamed x2, waiting for transfers between devices  182 us
    scatter-add x1, other arithmetic, per_device(): landed = jnp.zeros((brick_z, columns), jnp.float32).at[:, target].add(jnp...  66.9 us
    ppermute x12, starting transfers between devices, with_halo(): lax.ppermute(lax.slice_in_dim(block, block.shape[dim] - width, None, axis...  36 us
    ppermute x12, starting transfers between devices, with_halo(): lax.ppermute(lax.slice_in_dim(block, 0, width, axis=dim), axis, backward)  29.2 us
    concatenate x5, other arithmetic, with_halo(): block = jnp.concatenate([low, block, high], axis=dim)  20.4 us
    all_to_all x1, starting transfers between devices, per_device(): lax.all_to_all(jnp.stack([well_sources] * lax.axis_size(('gx', 'gy'))), (...  16.9 us
    all_to_all x1, starting transfers between devices, per_device(): lax.all_to_all(smooth_y, ('gx', 'gy'), split_axis=0, concat_axis=1, tiled...  15.5 us
    ppermute x12, waiting for transfers between devices, with_halo(): lax.ppermute(lax.slice_in_dim(block, block.shape[dim] - width, None, axis...  15 us
  transfers between devices with their start and end apart: 28, of which 13 were waited for; matrix products, arithmetic and copies ran while one was open for 12% of the time, Pallas kernels for 0%

profile of v1, /device:TPU:1, one launch (start us, length us, event | category | flops | bytes accessed | tf_op | source)
XLA Modules:
  0.0 534.9 jit_solution(2173741415683931061)
XLA Ops:
  9.6 16.9 %all-to-all-start = ((f32[128,96,32]{1,2,0:T(8,128)}), f32[128,96,32]{1,2,0:T(8,128)}, u32[]{:S(2)}, u32[]{:S(2)}) async-start(f32[128,96,32]{1,2,0:T(8,128)} %stack.12), calls=%async_computation | async-start | bytes 4194304 | tf_op jit(solution)/shard_map/all_to_all | solution.py:58
  37.4 8.2 %collective-permute-done = f32[2,3,3,32,1,128]{5,3,4,2,1,0:T(8,128)S(1)} collective-permute-done((f32[2,3,3,32,1,128]{5,3,4,2,1,0:T(8,128)}, f32[2,3,3,32,1,128]{5,3,4,2,1,0:T(8,128)S(1)}, u32[]{:S(2)}, u32[]{:S(2)}) %collective-permute-start) | collective-permute-done | bytes 294944 | tf_op jit(solution)/shard_map/ppermute | solution.py:15
  51.0 6.3 %fusion.95 = (f32[2,3,3,32,18,1]{5,3,4,2,1,0:T(8,128)}, f32[2,3,3,32,18,1]{5,3,4,2,1,0:T(8,128)}) fusion(f32[2,3,3,32,18,128]{5,3,4,2,1,0:T(8,128)S(1)} %pad_maximum_fusion.1), kind=kLoop, calls=%fused_computation.232 | loop fusion | bytes 165888 | tf_op jit(solution)/shard_map/slice | solution.py:16
  63.6 4.4 copy.70
  69.5 181.7 %all-reduce.5.cloned.1.call-done = (s32[12288]{0:T(1024)}, s32[12288]{0:T(1024)}) async-done(((s32[12288]{0:T(1024)}, s32[12288]{0:T(1024)}), (s32[12288]{0:T(1024)}, s32[12288]{0:T(1024)})) %all-reduce.5.cloned.1.call-update) | async-done | bytes 98320
  255.7 4.4 copy.72
  260.1 5.3 copy.88
  265.5 66.9 %scatter_custom_fusion = f32[32,2048]{0,1:T(8,128)} fusion(s32[12288]{0:T(1024)S(1)} %compare_select_fusion, f32[12288,32]{1,0:T(8,128)} %bitcast.159, f32[]{:T(128)} %constant.79.clone.1), kind=kCustom, calls=%fused_computation.47 | custom fusion | flops 393216 | bytes 262656 | tf_op jit(solution)/shard_map/scatter-add | solution.py:70
  335.3 4.5 collective-permute-start.7
  339.8 6.5 %pad_maximum_fusion.7 = (f32[2,3,3,1,18,130]{5,3,4,2,1,0:T(1,128)S(1)}, f32[2,3,3,1,18,130]{5,3,4,2,1,0:T(1,128)S(1)}) fusion(f32[2,3,3,32,18,1]{5,3,4,2,1,0:T(8,128)} %copy.72, f32[2,3,3,32,18,1]{5,3,4,2,1,0:T(8,128)} %copy.71, f32[2,3,3,32,1,128]{5,3,4,2,1,0:T(8,128)} %collective-permute-done.1, f32[2,3,3,32,1,128]{5,3,4,2,1,0:T(8,128)} %copy-done.2, ...), kind=kLoop, calls=%fused_computation.55 | loop fusion | flops 421200 | bytes 5728320 | tf_op jit(solution)/shard_map/slice | solution.py:16
  347.6 7.6 %collective-permute-start.5 = (f32[2,3,3,1,18,130]{5,3,4,2,1,0:T(1,128)S(1)}, f32[2,3,3,1,18,130]{5,3,4,2,1,0:T(1,128)S(1)}, u32[]{:S(2)}, u32[]{:S(2)}) collective-permute-start(f32[2,3,3,1,18,130]{5,3,4,2,1,0:T(1,128)S(1)} %get-tuple-element.13), channel_id=1, source_target_pairs={{1,0},{3,2},{5,4},{7,6},{9,8},{11,10},{13,12},{15,14},{17,16},{19,... | collective-permute-start | bytes 505448 | tf_op jit(solution)/shard_map/ppermute | solution.py:18
  360.8 17.7 %pad_maximum_fusion = f32[2,3,3,34,18,130]{5,3,4,2,1,0:T(8,128)} fusion(f32[2,3,3,1,18,130]{5,3,4,2,1,0:T(1,128)S(1)} %collective-permute-done.5, f32[2,3,3,32,18,1]{5,3,4,2,1,0:T(8,128)S(1)} %bitcast.157, f32[2,3,3,32,1,128]{5,3,4,2,1,0:T(8,128)} %collective-permute-done.1, f32[1,3,3,32,16,128]{5,3,4,2,1,0:T(8,128)S(1)} %copy-done.1, ...), kind=kLoop, calls=%fused_computation.1 | loop fusion | flops 10024560 | bytes 11456640 | tf_op jit(solution)/shard_map/concatenate | solution.py:19
  382.1 9.0 %slice_bitcast_fusion.1 = (f32[3,34,18,130]{3,1,2,0:T(8,128)S(1)}, f32[3,34,18,130]{3,1,2,0:T(8,128)}, f32[3,34,18,130]{3,1,2,0:T(8,128)}, f32[3,34,18,130]{3,1,...) fusion(f32[2,3,3,34,18,130]{5,3,4,2,1,0:T(8,128)} %pad_maximum_fusion), kind=kLoop, calls=%fused_computation.13 | loop fusion | bytes 11456640 | tf_op jit(solution)/shard_map/squeeze | solution.py:81
  409.8 5.5 %collective-permute-start.16 = (f32[1,18,130]{2,0,1:T(1,128)S(1)}, f32[1,18,130]{2,0,1:T(1,128)S(1)}, u32[]{:S(2)}, u32[]{:S(2)}) collective-permute-start(f32[1,18,130]{2,0,1:T(1,128)S(1)} %get-tuple-element.28), channel_id=1, source_target_pairs={{1,0},{3,2},{5,4},{7,6},{9,8},{11,10},{13,12},{15,14},{17,16},{19,... | collective-permute-start | bytes 28088 | tf_op jit(solution)/shard_map/ppermute | solution.py:18
  429.1 4.8 collective-permute-start.21
  433.9 4.4 collective-permute-done.20
  449.1 9.2 %all-to-all-start.1 = ((f32[32,16,128]{2,0,1:T(8,128)}), f32[32,16,128]{2,0,1:T(8,128)S(1)}, u32[]{:S(2)}, u32[]{:S(2)}) async-start(f32[32,16,128]{2,0,1:T(8,128)} %get-tuple-element.8), calls=%async_computation.1 | async-start | bytes 524288 | tf_op jit(solution)/shard_map/all_to_all | solution.py:84
  458.4 12.2 %all-to-all-done.1 = f32[32,16,128]{2,0,1:T(8,128)S(1)} async-done(((f32[32,16,128]{2,0,1:T(8,128)}), f32[32,16,128]{2,0,1:T(8,128)S(1)}, u32[]{:S(2)}, u32[]{:S(2)}) %all-to-all-start.1) | async-done | bytes 262176 | tf_op jit(solution)/shard_map/all_to_all | solution.py:84
  470.8 5.0 fusion
  477.1 15.5 %all-to-all-start.2 = ((f32[128,1,512]{2,1,0:T(1,128)}), f32[128,1,512]{2,1,0:T(1,128)S(1)}, u32[]{:S(2)}, u32[]{:S(2)}) async-start(f32[128,1,512]{2,1,0:T(1,128)} %reshape.202), calls=%async_computation.2 | async-start | bytes 524288 | tf_op jit(solution)/shard_map/all_to_all | solution.py:96
  493.5 12.8 %all-to-all-done.2 = f32[128,1,512]{2,1,0:T(1,128)S(1)} async-done(((f32[128,1,512]{2,1,0:T(1,128)}), f32[128,1,512]{2,1,0:T(1,128)S(1)}, u32[]{:S(2)}, u32[]{:S(2)}) %all-to-all-start.2) | async-done | bytes 262176 | tf_op jit(solution)/shard_map/all_to_all | solution.py:96
  508.6 5.6 %all_to_all.49 = f32[2,4,8192]{2,1,0:T(4,128)S(1)} all-to-all(f32[2,4,8192]{2,1,0:T(4,128)S(1)} %all_to_all.42), channel_id=1, replica_groups=mesh['gx'=16,'gy'=8,'gz'=2] {'gz'}, dimensions={0} | all-to-all | bytes 524288 | tf_op jit(solution)/shard_map/all_to_all | solution.py:95
  514.2 5.0 copy.84
  519.2 7.2 %copy.85 = f32[4,2,32,2,128]{4,2,1,3,0:T(8,128)S(1)} copy(f32[4,2,32,2,128]{0,3,2,4,1:T(2,128)} %bitcast.158) | data formatting | bytes 524288 | tf_op jit(solution)/shard_map/ykdza,jda->ykzj/dot_general | solution.py:107
  (131 shorter events, 92.8 us)
Async XLA Ops:
  9.6 250.5 %all-to-all-start = ((f32[128,96,32]{1,2,0:T(8,128)}), f32[128,96,32]{1,2,0:T(8,128)}, u32[]{:S(2)}, u32[]{:S(2)}) async-start(f32[128,96,32]{1,2,0:T(8,128)} %stack.12), calls=%async_computation | async-start | bytes 4194304 | tf_op jit(solution)/shard_map/all_to_all | solution.py:58
  26.5 224.8 %all-reduce.5.cloned.1.call-start = ((), (), s32[]{:S(2)}) async-start(), calls=%async_computation.4 | async-start | bytes 196608
  31.4 14.2 %collective-permute-start = (f32[2,3,3,32,1,128]{5,3,4,2,1,0:T(8,128)}, f32[2,3,3,32,1,128]{5,3,4,2,1,0:T(8,128)S(1)}, u32[]{:S(2)}, u32[]{:S(2)}) collective-permute-start(f32[2,3,3,32,1,128]{5,3,4,2,1,0:T(8,128)} %get-tuple-element.22), channel_id=1, source_target_pairs={{0,16},{16,32},{32,48},{48,64},{64,80},{80,96},{96,112},{112,128},... | collective-permute-start | bytes 884744 | tf_op jit(solution)/shard_map/ppermute | solution.py:15
  33.8 14.6 %collective-permute-start.1 = (f32[2,3,3,32,1,128]{5,3,4,2,1,0:T(8,128)}, f32[2,3,3,32,1,128]{5,3,4,2,1,0:T(8,128)}, u32[]{:S(2)}, u32[]{:S(2)}) collective-permute-start(f32[2,3,3,32,1,128]{5,3,4,2,1,0:T(8,128)} %get-tuple-element.23), channel_id=1, source_target_pairs={{16,0},{32,16},{48,32},{64,48},{80,64},{96,80},{112,96},{128,112},... | collective-permute-start | bytes 884744 | tf_op jit(solution)/shard_map/ppermute | solution.py:18
  61.1 190.9 %collective-permute-start.2 = (f32[2,3,3,32,18,1]{3,0,5,4,2,1:T(2,128)S(1)}, f32[2,3,3,32,18,1]{3,0,5,4,2,1:T(2,128)S(1)}, u32[]{:S(2)}, u32[]{:S(2)}) collective-permute-start(f32[2,3,3,32,18,1]{3,0,5,4,2,1:T(2,128)S(1)} %copy.69), channel_id=1, source_target_pairs={{0,2},{2,4},{4,6},{6,8},{8,10},{10,12},{12,14},{1,3},{3,5},{5,7},{... | collective-permute-start | bytes 124424 | tf_op jit(solution)/shard_map/ppermute | solution.py:15
  68.0 187.7 %collective-permute-start.3 = (f32[2,3,3,32,18,1]{3,0,5,4,2,1:T(2,128)}, f32[2,3,3,32,18,1]{3,0,5,4,2,1:T(2,128)}, u32[]{:S(2)}, u32[]{:S(2)}) collective-permute-start(f32[2,3,3,32,18,1]{3,0,5,4,2,1:T(2,128)} %copy.70), channel_id=1, source_target_pairs={{2,0},{4,2},{6,4},{8,6},{10,8},{12,10},{14,12},{3,1},{5,3},{7,5},{... | collective-permute-start | bytes 124424 | tf_op jit(solution)/shard_map/ppermute | solution.py:18
  334.0 21.2 %collective-permute-start.6 = (f32[32,1,128]{2,0,1:T(8,128)S(1)}, f32[32,1,128]{2,0,1:T(8,128)S(1)}, u32[]{:S(2)}, u32[]{:S(2)}) collective-permute-start(f32[32,1,128]{2,0,1:T(8,128)S(1)} %get-tuple-element.49), channel_id=1, source_target_pairs={{16,0},{32,16},{48,32},{64,48},{80,64},{96,80},{112,96},{128,112},... | collective-permute-start | bytes 49160 | tf_op jit(solution)/shard_map/ppermute | solution.py:18
  335.3 19.9 %collective-permute-start.7 = (f32[32,1,128]{2,0,1:T(8,128)S(1)}, f32[32,1,128]{2,0,1:T(8,128)S(1)}, u32[]{:S(2)}, u32[]{:S(2)}) collective-permute-start(f32[32,1,128]{2,0,1:T(8,128)S(1)} %get-tuple-element.48), channel_id=1, source_target_pairs={{0,16},{16,32},{32,48},{48,64},{64,80},{80,96},{96,112},{112,128},... | collective-permute-start | bytes 49160 | tf_op jit(solution)/shard_map/ppermute | solution.py:15
  346.3 14.4 %collective-permute-start.4 = (f32[2,3,3,1,18,130]{5,3,4,2,1,0:T(1,128)S(1)}, f32[2,3,3,1,18,130]{5,3,4,2,1,0:T(1,128)S(1)}, u32[]{:S(2)}, u32[]{:S(2)}) collective-permute-start(f32[2,3,3,1,18,130]{5,3,4,2,1,0:T(1,128)S(1)} %get-tuple-element.12), channel_id=1, source_target_pairs={{0,1},{2,3},{4,5},{6,7},{8,9},{10,11},{12,13},{14,15},{16,17},{18,... | collective-permute-start | bytes 505448 | tf_op jit(solution)/shard_map/ppermute | solution.py:15
  347.6 13.1 %collective-permute-start.5 = (f32[2,3,3,1,18,130]{5,3,4,2,1,0:T(1,128)S(1)}, f32[2,3,3,1,18,130]{5,3,4,2,1,0:T(1,128)S(1)}, u32[]{:S(2)}, u32[]{:S(2)}) collective-permute-start(f32[2,3,3,1,18,130]{5,3,4,2,1,0:T(1,128)S(1)} %get-tuple-element.13), channel_id=1, source_target_pairs={{1,0},{3,2},{5,4},{7,6},{9,8},{11,10},{13,12},{15,14},{17,16},{19,... | collective-permute-start | bytes 505448 | tf_op jit(solution)/shard_map/ppermute | solution.py:18
  355.4 23.1 %collective-permute-start.8 = (f32[32,18,1]{2,0,1:T(8,128)S(1)}, f32[32,18,1]{2,0,1:T(8,128)S(1)}, u32[]{:S(2)}, u32[]{:S(2)}) collective-permute-start(f32[32,18,1]{2,0,1:T(8,128)S(1)} %get-tuple-element.43), channel_id=1, source_target_pairs={{2,0},{4,2},{6,4},{8,6},{10,8},{12,10},{14,12},{3,1},{5,3},{7,5},{... | collective-permute-start | bytes 6920 | tf_op jit(solution)/shard_map/ppermute | solution.py:18
  356.7 21.8 %collective-permute-start.9 = (f32[32,18,1]{2,0,1:T(8,128)S(1)}, f32[32,18,1]{2,0,1:T(8,128)S(1)}, u32[]{:S(2)}, u32[]{:S(2)}) collective-permute-start(f32[32,18,1]{2,0,1:T(8,128)S(1)} %get-tuple-element.42), channel_id=1, source_target_pairs={{0,2},{2,4},{4,6},{6,8},{8,10},{10,12},{12,14},{1,3},{3,5},{5,7},{... | collective-permute-start | bytes 6920 | tf_op jit(solution)/shard_map/ppermute | solution.py:15
  378.7 12.4 %collective-permute-start.10 = (f32[1,18,130]{2,0,1:T(1,128)S(1)}, f32[1,18,130]{2,0,1:T(1,128)S(1)}, u32[]{:S(2)}, u32[]{:S(2)}) collective-permute-start(f32[1,18,130]{2,0,1:T(1,128)S(1)} %get-tuple-element.30), channel_id=1, source_target_pairs={{1,0},{3,2},{5,4},{7,6},{9,8},{11,10},{13,12},{15,14},{17,16},{19,... | collective-permute-start | bytes 28088 | tf_op jit(solution)/shard_map/ppermute | solution.py:18
  380.6 10.5 %collective-permute-start.11 = (f32[1,18,130]{2,0,1:T(1,128)S(1)}, f32[1,18,130]{2,0,1:T(1,128)S(1)}, u32[]{:S(2)}, u32[]{:S(2)}) collective-permute-start(f32[1,18,130]{2,0,1:T(1,128)S(1)} %get-tuple-element.31), channel_id=1, source_target_pairs={{0,1},{2,3},{4,5},{6,7},{8,9},{10,11},{12,13},{14,15},{16,17},{18,... | collective-permute-start | bytes 28088 | tf_op jit(solution)/shard_map/ppermute | solution.py:15
  394.2 5.4 %collective-permute-start.12 = (f32[32,1,128]{2,0,1:T(8,128)S(1)}, f32[32,1,128]{2,0,1:T(8,128)S(1)}, u32[]{:S(2)}, u32[]{:S(2)}) collective-permute-start(f32[32,1,128]{2,0,1:T(8,128)S(1)} %get-tuple-element.47), channel_id=1, source_target_pairs={{16,0},{32,16},{48,32},{64,48},{80,64},{96,80},{112,96},{128,112},... | collective-permute-start | bytes 49160 | tf_op jit(solution)/shard_map/ppermute | solution.py:18
  400.7 8.2 %collective-permute-start.14 = (f32[32,18,1]{2,0,1:T(8,128)S(1)}, f32[32,18,1]{2,0,1:T(8,128)S(1)}, u32[]{:S(2)}, u32[]{:S(2)}) collective-permute-start(f32[32,18,1]{2,0,1:T(8,128)S(1)} %get-tuple-element.41), channel_id=1, source_target_pairs={{2,0},{4,2},{6,4},{8,6},{10,8},{12,10},{14,12},{3,1},{5,3},{7,5},{... | collective-permute-start | bytes 6920 | tf_op jit(solution)/shard_map/ppermute | solution.py:18
  402.0 7.6 %collective-permute-start.15 = (f32[32,18,1]{2,0,1:T(8,128)S(1)}, f32[32,18,1]{2,0,1:T(8,128)S(1)}, u32[]{:S(2)}, u32[]{:S(2)}) collective-permute-start(f32[32,18,1]{2,0,1:T(8,128)S(1)} %get-tuple-element.40), channel_id=1, source_target_pairs={{0,2},{2,4},{4,6},{6,8},{8,10},{10,12},{12,14},{1,3},{3,5},{5,7},{... | collective-permute-start | bytes 6920 | tf_op jit(solution)/shard_map/ppermute | solution.py:15
  409.8 6.8 %collective-permute-start.16 = (f32[1,18,130]{2,0,1:T(1,128)S(1)}, f32[1,18,130]{2,0,1:T(1,128)S(1)}, u32[]{:S(2)}, u32[]{:S(2)}) collective-permute-start(f32[1,18,130]{2,0,1:T(1,128)S(1)} %get-tuple-element.28), channel_id=1, source_target_pairs={{1,0},{3,2},{5,4},{7,6},{9,8},{11,10},{13,12},{15,14},{17,16},{19,... | collective-permute-start | bytes 28088 | tf_op jit(solution)/shard_map/ppermute | solution.py:18
  421.1 5.7 %collective-permute-start.18 = (f32[32,1,128]{2,0,1:T(8,128)S(1)}, f32[32,1,128]{2,0,1:T(8,128)S(1)}, u32[]{:S(2)}, u32[]{:S(2)}) collective-permute-start(f32[32,1,128]{2,0,1:T(8,128)S(1)} %get-tuple-element.45), channel_id=1, source_target_pairs={{16,0},{32,16},{48,32},{64,48},{80,64},{96,80},{112,96},{128,112},... | collective-permute-start | bytes 49160 | tf_op jit(solution)/shard_map/ppermute | solution.py:18
  422.4 5.2 collective-permute-start.19
  427.8 10.5 %collective-permute-start.20 = (f32[32,18,1]{2,0,1:T(8,128)S(1)}, f32[32,18,1]{2,0,1:T(8,128)S(1)}, u32[]{:S(2)}, u32[]{:S(2)}) collective-permute-start(f32[32,18,1]{2,0,1:T(8,128)S(1)} %get-tuple-element.39), channel_id=1, source_target_pairs={{2,0},{4,2},{6,4},{8,6},{10,8},{12,10},{14,12},{3,1},{5,3},{7,5},{... | collective-permute-start | bytes 6920 | tf_op jit(solution)/shard_map/ppermute | solution.py:18
  429.1 10.1 %collective-permute-start.21 = (f32[32,18,1]{2,0,1:T(8,128)S(1)}, f32[32,18,1]{2,0,1:T(8,128)S(1)}, u32[]{:S(2)}, u32[]{:S(2)}) collective-permute-start(f32[32,18,1]{2,0,1:T(8,128)S(1)} %get-tuple-element.38), channel_id=1, source_target_pairs={{0,2},{2,4},{4,6},{6,8},{8,10},{10,12},{12,14},{1,3},{3,5},{5,7},{... | collective-permute-start | bytes 6920 | tf_op jit(solution)/shard_map/ppermute | solution.py:15
  449.1 21.5 %all-to-all-start.1 = ((f32[32,16,128]{2,0,1:T(8,128)}), f32[32,16,128]{2,0,1:T(8,128)S(1)}, u32[]{:S(2)}, u32[]{:S(2)}) async-start(f32[32,16,128]{2,0,1:T(8,128)} %get-tuple-element.8), calls=%async_computation.1 | async-start | bytes 524288 | tf_op jit(solution)/shard_map/all_to_all | solution.py:84
  477.1 29.2 %all-to-all-start.2 = ((f32[128,1,512]{2,1,0:T(1,128)}), f32[128,1,512]{2,1,0:T(1,128)S(1)}, u32[]{:S(2)}, u32[]{:S(2)}) async-start(f32[128,1,512]{2,1,0:T(1,128)} %reshape.202), calls=%async_computation.2 | async-start | bytes 524288 | tf_op jit(solution)/shard_map/all_to_all | solution.py:96
  (22 other events, 289.9 us)
Sparse Core Ops, SparseCore 0:
  37.5 213.6 all-reduce.4
